TPU v7x, 512 devices: a whole 4x4x16 slice. The times are simulated.
512 devices in a mesh: shard: 128 (over z, y, core), tensor: 4 (over x).
Axes of the slice: x: 4, y: 4, z: 16, core: 2. Of those that a mesh axis runs over, the one named last changes fastest.
Arguments:
- wo_grads: bfloat16 [4, 2, 8, 8, 512, 512], P('tensor', None, None, None, 'shard'), may hold values from -6 to 6
- wo_master: float32 [2, 8, 8, 512, 512], P(None, None, None, 'shard', 'tensor'), may hold values from -0.09375 to 0.09375
- left_stats: float32 [256, 512, 512], P('shard', 'tensor'), may hold values from -6 to 6
- right_stats: float32 [256, 512, 512], P('shard', 'tensor'), may hold values from -6 to 6
- left_roots: bfloat16 [256, 512, 512], P('shard', 'tensor'), as said below
- right_roots: bfloat16 [256, 512, 512], P('shard', 'tensor'), as said below
- row_moments: float32 [256, 512], P('shard'), may hold values from 0.003 to 0.05
- col_moments: float32 [256, 512], P('shard'), may hold values from 0.002 to 0.1
- owners: int32 [128], replicated, may hold values from 0 to 127, as said below
- emb_grads: bfloat16 [4, 4096, 4096], P('tensor', 'shard'), may hold values from -3 to 3
- emb_master: float32 [4096, 4096], P('shard', 'tensor'), may hold values from -0.75 to 0.75
- emb_mean: float32 [4096, 4096], P('shard', 'tensor'), may hold values from -0.75 to 0.75
- emb_var: float32 [4096, 4096], P('shard', 'tensor'), may hold values from 0.002 to 0.05
- gain_grads: bfloat16 [4, 2, 4096], P('tensor', None, 'shard'), may hold values from -3 to 3
- gain_master: float32 [2, 4096], P(None, ('shard', 'tensor')), may hold values from 0.5 to 1.5
- gain_mean: float32 [2, 4096], P(None, ('shard', 'tensor')), may hold values from -0.75 to 0.75
- gain_var: float32 [2, 4096], P(None, ('shard', 'tensor')), may hold values from 0.002 to 0.05
Outputs:
- wo_new: float32 [2, 8, 8, 512, 512], P(None, None, None, 'shard', 'tensor')
- wo_weights: bfloat16 [2, 8, 8, 512, 512], P(None, None, None, 'shard')
- left_new: float32 [256, 512, 512], P('shard', 'tensor')
- right_new: float32 [256, 512, 512], P('shard', 'tensor')
- row_new: float32 [256, 512], P('shard')
- col_new: float32 [256, 512], P('shard')
- emb_new: float32 [4096, 4096], P('shard', 'tensor')
- emb_mean_new: float32 [4096, 4096], P('shard', 'tensor')
- emb_var_new: float32 [4096, 4096], P('shard', 'tensor')
- emb_weights: bfloat16 [4096, 4096], P('shard')
- gain_new: float32 [2, 4096], P(None, ('shard', 'tensor'))
- gain_mean_new: float32 [2, 4096], P(None, ('shard', 'tensor'))
- gain_var_new: float32 [2, 4096], P(None, ('shard', 'tensor'))
- gain_weights: bfloat16 [2, 4096], P(None, 'shard')
Inputs may be any that keep to these rules, and one draw needn't show every extreme that they name: `owners`: each index of shard owns at most 2 of the 128 blocks, and some index owns exactly 2. `left_roots`: each slot's matrix is symmetric. `right_roots`: each slot's matrix is symmetric.
All inputs are finite; a program needn't handle non-finite values.
Results may differ from a plain program's by a relative error of at most 0.0052.
Values may be sent and summed in bfloat16 or wider, within the bound.
No kernel may reach another device: no remote copies, remote signals or barrier semaphores. Data moves between devices by JAX's collectives and lax.ppermute only.
A program may use at most 128 MiB of HBM per device.

v0:
```python
import jax
import jax.numpy as jnp
from jax import lax
from jax.sharding import PartitionSpec as P

beta_one = 0.9
beta_two = 0.95
bias_one = 1.0 - 0.9**10
bias_two = 1.0 - 0.95**10
adam_eps = 1e-08
learn_rate = 0.01
decay_rate = 0.1
graft_eps = 1e-06
factor_eps = 1e-08
highest = lax.Precision.HIGHEST


def slot_table(owners, slot_count, owner_count):
    block_ids = jnp.arange(owners.shape[0], dtype=jnp.int32)
    earlier = (owners[:, None] == owners[None, :]) & (block_ids[None, :] < block_ids[:, None])
    owner_rank = jnp.sum(earlier.astype(jnp.int32), axis=1)
    slot_of = owners * slot_count + owner_rank
    slot_ids = jnp.arange(slot_count * owner_count, dtype=jnp.int32)
    slot_hits = (slot_of[:, None] == slot_ids[None, :]).astype(jnp.int32)
    block_of = jnp.sum(slot_hits * block_ids[:, None], axis=0)
    slot_used = jnp.sum(slot_hits, axis=0)
    return (slot_of, block_of, slot_used)


def adamw_step(gradient, master, first_moment, second_moment):
    mean_new = beta_one * first_moment + (1.0 - beta_one) * gradient
    var_new = beta_two * second_moment + (1.0 - beta_two) * gradient * gradient
    adam_dir = mean_new / bias_one / (jnp.sqrt(var_new / bias_two) + adam_eps)
    master_new = master - learn_rate * (adam_dir + decay_rate * master)
    return (master_new, mean_new, var_new, master_new.astype(jnp.bfloat16))


def per_device(
    wo_grads,
    wo_master,
    left_stats,
    right_stats,
    left_roots,
    right_roots,
    row_moments,
    col_moments,
    owners,
    emb_grads,
    emb_master,
    emb_mean,
    emb_var,
    gain_grads,
    gain_master,
    gain_mean,
    gain_var,
):
    micro_count = lax.axis_size("tensor")
    owner_count = lax.axis_size("shard")
    tensor_pos = lax.axis_index("tensor")
    slot_count = left_stats.shape[0]
    quarter = left_stats.shape[1]
    slot_of, block_of, slot_used = slot_table(owners, slot_count, owner_count)
    left_full = lax.all_gather(left_roots, "tensor", axis=1, tiled=True)
    emb_terms = emb_grads[0].astype(jnp.float32)
    gain_terms = gain_grads[0].astype(jnp.float32)
    wo_terms = wo_grads[0].astype(jnp.float32)
    wo_sum, emb_sum, gain_sum = (
        lax.psum_scatter(wo_terms, "tensor", scatter_dimension=4, tiled=True),
        lax.psum_scatter(emb_terms, "tensor", scatter_dimension=1, tiled=True),
        lax.psum_scatter(gain_terms, "tensor", scatter_dimension=1, tiled=True),
    )
    wo_mean = wo_sum / micro_count
    rows_dev = wo_mean.shape[3]
    flattened = wo_mean.reshape(-1, rows_dev, quarter)
    taken = jnp.take(flattened, block_of, axis=0)
    outgoing = jnp.where(slot_used[:, None, None] > 0, taken, 0.0)
    outgoing = outgoing.reshape(owner_count, slot_count, rows_dev, quarter)
    own_cols = lax.all_to_all(outgoing, "shard", split_axis=0, concat_axis=2, tiled=True)[0]
    full_block = lax.all_gather(own_cols, "tensor", axis=2, tiled=True)
    own_rows = lax.dynamic_slice_in_dim(full_block, tensor_pos * quarter, quarter, 1)
    left_new = left_stats + jnp.einsum("sqj,sij->sqi", own_rows, full_block, precision=highest)
    right_new = right_stats + jnp.einsum("siq,sij->sqj", own_cols, full_block, precision=highest)
    squares = full_block * full_block
    row_new = beta_two * row_moments + (1.0 - beta_two) * jnp.mean(squares, axis=2)
    col_new = beta_two * col_moments + (1.0 - beta_two) * jnp.mean(squares, axis=1)
    row_level = jnp.mean(row_new, axis=1)
    col_part = lax.dynamic_slice_in_dim(col_new, tensor_pos * quarter, quarter, 1)
    second_est = row_new[:, :, None] * col_part[:, None, :] / row_level[:, None, None]
    adam_dir = own_cols / (jnp.sqrt(second_est) + factor_eps)
    adam_part = jnp.sum(adam_dir * adam_dir, axis=(1, 2))
    adam_total = lax.psum(adam_part, "tensor")
    right_half = jnp.einsum(
        "sij,sqj->siq",
        full_block.astype(jnp.bfloat16),
        right_roots,
        preferred_element_type=jnp.float32,
    ).astype(jnp.bfloat16)
    shampoo = jnp.einsum("sik,skq->siq", left_full, right_half, preferred_element_type=jnp.float32)
    shampoo_part = jnp.sum(shampoo * shampoo, axis=(1, 2))
    shampoo_total = lax.psum(shampoo_part, "tensor")
    graft_ratio = jnp.sqrt(adam_total) / (jnp.sqrt(shampoo_total) + graft_eps)
    update = shampoo * graft_ratio[:, None, None]
    returned = lax.all_to_all(update, "shard", split_axis=1, concat_axis=0, tiled=True)
    local_update = jnp.take(returned, slot_of, axis=0).reshape(wo_master.shape)
    wo_new = wo_master - learn_rate * (local_update + decay_rate * wo_master)
    emb_grad = emb_sum / micro_count
    gain_grad = gain_sum / micro_count
    emb_new, emb_mean_new, emb_var_new, emb_low = adamw_step(
        emb_grad, emb_master, emb_mean, emb_var
    )
    gain_new, gain_mean_new, gain_var_new, gain_low = adamw_step(
        gain_grad, gain_master, gain_mean, gain_var
    )
    wo_weights, emb_weights, gain_weights = (
        lax.all_gather(wo_new.astype(jnp.bfloat16), "tensor", axis=4, tiled=True),
        lax.all_gather(emb_low, "tensor", axis=1, tiled=True),
        lax.all_gather(gain_low, "tensor", axis=1, tiled=True),
    )
    return (
        wo_new,
        wo_weights,
        left_new,
        right_new,
        row_new,
        col_new,
        emb_new,
        emb_mean_new,
        emb_var_new,
        emb_weights,
        gain_new,
        gain_mean_new,
        gain_var_new,
        gain_weights,
    )


def solution(mesh):
    in_specs = (
        P("tensor", None, None, None, "shard", None),
        P(None, None, None, "shard", "tensor"),
        P("shard", "tensor", None),
        P("shard", "tensor", None),
        P("shard", "tensor", None),
        P("shard", "tensor", None),
        P("shard", None),
        P("shard", None),
        P(),
        P("tensor", "shard", None),
        P("shard", "tensor"),
        P("shard", "tensor"),
        P("shard", "tensor"),
        P("tensor", None, "shard"),
        P(None, ("shard", "tensor")),
        P(None, ("shard", "tensor")),
        P(None, ("shard", "tensor")),
    )
    out_specs = (
        P(None, None, None, "shard", "tensor"),
        P(None, None, None, "shard", None),
        P("shard", "tensor", None),
        P("shard", "tensor", None),
        P("shard", None),
        P("shard", None),
        P("shard", "tensor"),
        P("shard", "tensor"),
        P("shard", "tensor"),
        P("shard", None),
        P(None, ("shard", "tensor")),
        P(None, ("shard", "tensor")),
        P(None, ("shard", "tensor")),
        P(None, "shard"),
    )
    return jax.shard_map(
        per_device, mesh=mesh, in_specs=in_specs, out_specs=out_specs, check_vma=False
    )
```

profile of v0, /device:TPU:40, one launch (start us, length us, event | category | flops | bytes accessed | tf_op | source)
XLA Modules:
  0.0 324.4 jit_solution(10380883053698371560)
XLA Ops:
  7.2 1.2 bitcast_convert_fusion
  8.5 26.2 %copy.74 = f32[2,8,8,4,512]{3,2,1,0,4:T(8,128)} copy(f32[2,8,8,4,512]{4,3,2,1,0:T(4,128)S(1)} %bitcast_convert_fusion) | data formatting | bytes 2097152
  34.7 29.3 %reshape.124 = f32[512,512]{1,0:T(8,128)} reshape(f32[512,2,8,8,4]{4,3,2,1,0:T(8,128)} %bitcast.45) | data formatting | bytes 2097152
  64.1 0.2 convert_reduce_fusion.1
  64.3 0.5 compare_and_fusion.1
  64.8 0.1 convert_reduce_fusion
  64.9 0.4 copy-done.12
  65.3 0.1 reduce_sum.79
  65.5 0.2 gt.18
  65.7 33.9 %reduce-scatter.8.cloned.1.call-done = f32[128,512]{1,0:T(8,128)} async-done(((f32[512,512]{1,0:T(8,128)}), f32[128,512]{1,0:T(8,128)}) %reduce-scatter.8.cloned.1.call-update) | async-done | bytes 262160
  99.6 10.8 %reshape.125 = f32[128,2,8,8,4]{4,3,2,1,0:T(8,128)} reshape(f32[128,512]{1,0:T(8,128)} %reduce-scatter.8.cloned.1.call-done) | data formatting | bytes 524288
  110.5 6.6 %copy.75 = f32[2,8,8,4,128]{4,3,2,1,0:T(4,128)S(1)} copy(f32[2,8,8,4,128]{3,2,1,0,4:T(8,128)} %bitcast.46) | data formatting | bytes 524288
  117.2 1.0 gather_fusion
  118.2 0.5 select_select_fusion
  118.8 0.2 copy.61
  119.0 48.5 %all_to_all.33 = f32[128,2,4,128]{3,1,2,0:T(2,128)S(1)} all-to-all(f32[128,2,4,128]{3,1,2,0:T(2,128)S(1)} %copy.61), channel_id=1, replica_groups=mesh['shard'=128,'tensor'=4] {'shard'}, dimensions={0} | all-to-all | bytes 1048576 | tf_op jit(solution)/shard_map/all_to_all | solution.py:78
  167.5 0.9 copy.62
  168.5 0.7 all-gather.6.cloned.1.call-update
  169.2 0.8 bitcast_convert_fusion.1
  170.1 0.6 bitcast_convert_fusion.2
  170.6 30.6 %all-gather.4.cloned.1.call-done = f32[2,512,512]{2,1,0:T(8,128)} async-done(((f32[2,512,128]{2,1,0:T(8,128)}), f32[2,512,512]{2,1,0:T(8,128)}) %all-gather.4.cloned.1.call-update) | async-done | bytes 2097168 | tf_op jit(solution)/shard_map/all_gather | solution.py:79
  201.2 2.0 multiply_reduce_fusion
  203.3 0.1 fusion.8
  203.4 0.9 copy.73
  204.3 0.5 broadcast_multiply_fusion.1
  204.8 31.3 %all-gather.6.cloned.1.call-done = bf16[2,512,512]{2,1,0:T(8,128)(2,1)} async-done(((bf16[2,128,512]{2,1,0:T(8,128)(2,1)}), bf16[2,512,512]{2,1,0:T(8,128)(2,1)}) %all-gather.6.cloned.1.call-update) | async-done | bytes 1048592 | tf_op jit(solution)/shard_map/all_gather | solution.py:63
  236.1 2.2 multiply_reduce_fusion.2
  238.3 2.3 multiply_reduce_fusion.3
  240.6 10.0 %all-reduce.1 = (f32[2]{0:T(128)S(1)}, f32[2]{0:T(128)S(1)}, f32[2,32]{1,0:T(2,128)}) all-reduce(f32[2]{0:T(128)S(1)} %get-tuple-element.35, f32[2]{0:T(128)S(1)} %multiply_reduce_fusion.3, f32[2,32]{1,0:T(2,128)} %bitcast_convert_fusion.2), channel_id=1, replica_groups=mesh['shard'=128,'tensor'=4] {'tensor'}, use_global_device_ids=true, to_apply=%region_10.11 | all-reduce | flops 68 | bytes 544 | tf_op jit(solution)/shard_map/psum | solution.py:100
  250.6 0.1 multiply_bitcast_fusion
  250.7 1.0 copy.65
  251.7 16.6 %all-to-all-start.1 = ((f32[2,512,128]{2,0,1:T(2,128)}), f32[2,512,128]{2,0,1:T(2,128)S(1)}, u32[]{:S(2)}, u32[]{:S(2)}) async-start(f32[2,512,128]{2,0,1:T(2,128)} %copy.65), calls=%async_computation.1 | async-start | bytes 1048576 | tf_op jit(solution)/shard_map/all_to_all | solution.py:103
  268.3 0.7 broadcast_in_dim.48
  269.1 1.3 dynamic-slice
  271.1 1.9 fusion.6
  273.0 13.1 %all_gather.18 = bf16[32,4096]{1,0:T(8,128)(2,1)} all-gather(bf16[32,1024]{1,0:T(8,128)(2,1)S(1)} %get-tuple-element.25), channel_id=1, replica_groups=mesh['shard'=128,'tensor'=4] {'tensor'}, dimensions={1}, use_global_device_ids=true | all-gather | bytes 327680 | tf_op jit(solution)/shard_map/all_gather | solution.py:116
  286.1 1.4 convert_bitcast_fusion
  287.4 7.3 %all-gather = bf16[4,8,2]{1,2,0:T(2,128)(2,1)S(1)} all-gather(bf16[1,8,2]{1,2,0:T(2,128)(2,1)S(1)} %get-tuple-element.21), channel_id=1, replica_groups=mesh['shard'=128,'tensor'=4] {'tensor'}, dimensions={0}, use_global_device_ids=true | all-gather | bytes 160 | tf_op jit(solution)/shard_map/all_gather | solution.py:117
  294.8 0.6 reshape.123
  295.4 4.1 %convolution_add_fusion.1 = f32[2,128,512]{2,1,0:T(8,128)} fusion(f32[2,128,512]{2,1,0:T(8,128)} %param.19, f32[2,512,512]{2,1,0:T(8,128)S(1)} %copy-done.1, s32[]{:T(128)S(6)} %select_n.46), kind=kOutput, calls=%fused_computation.5 | convolution fusion | flops 805437440 | bytes 3670020 | tf_op jit(solution)/shard_map/sqj,sij->sqi/dot_general | solution.py:81
  299.5 2.2 convolution_add_fusion
  301.7 0.4 copy.67
  302.1 0.3 copy.68
  302.5 0.7 gather_fusion.1
  303.3 0.9 fusion.7
  304.2 12.2 %all_gather.17 = bf16[2,8,8,4,512]{4,3,2,1,0:T(4,128)(2,1)S(1)} all-gather(bf16[2,8,8,4,128]{4,3,2,1,0:T(4,128)(2,1)S(1)} %get-tuple-element.29), channel_id=1, replica_groups=mesh['shard'=128,'tensor'=4] {'tensor'}, dimensions={4}, use_global_device_ids=true | all-gather | bytes 655360 | tf_op jit(solution)/shard_map/all_gather | solution.py:115
  316.4 0.8 copy.80
  317.2 0.7 copy.81
  (56 shorter events, 0.5 us)
Async XLA Ops:
  7.2 229.0 %copy-start = (bf16[2,128,512]{2,1,0:T(8,128)(2,1)S(1)}, bf16[2,128,512]{2,1,0:T(8,128)(2,1)}, u32[]{:S(2)}) copy-start(bf16[2,128,512]{2,1,0:T(8,128)(2,1)} %param.22) | copy-start | bytes 786436
  7.2 92.5 %reduce-scatter.8.cloned.1.call-start = ((), (), s32[]{:S(2)}) async-start(), calls=%async_computation.7 | async-start | bytes 1310720
  34.7 29.4 %copy-start.16 = (s32[128]{0:T(128)S(1)}, s32[128]{0:T(128)}, u32[]{:S(2)}) copy-start(s32[128]{0:T(128)} %param.25) | copy-start | bytes 1540
  64.1 137.2 %all-gather.4.cloned.1.call-start = ((), (), s32[]{:S(2)}) async-start(), calls=%async_computation.4 | async-start | bytes 2621440 | tf_op jit(solution)/shard_map/all_gather | solution.py:79
  64.8 0.5 copy-start.12
  118.7 50.5 %copy-start.5 = (bf16[1,32,4096]{2,1,0:T(8,128)(2,1)S(1)}, bf16[1,32,4096]{2,1,0:T(8,128)(2,1)}, u32[]{:S(2)}) copy-start(bf16[1,32,4096]{2,1,0:T(8,128)(2,1)} %param.26) | copy-start | bytes 786436
  118.9 51.1 %copy-start.17 = (bf16[1,2,32]{2,1,0:T(2,128)(2,1)S(1)}, bf16[1,2,32]{2,1,0:T(2,128)(2,1)}, u32[]{:S(2)}) copy-start(bf16[1,2,32]{2,1,0:T(2,128)(2,1)} %param.30) | copy-start | bytes 388
  168.4 34.9 %copy-start.10 = (f32[2,512]{1,0:T(2,128)S(1)}, f32[2,512]{1,0:T(2,128)}, u32[]{:S(2)}) copy-start(f32[2,512]{1,0:T(2,128)} %param.23) | copy-start | bytes 12292
  168.4 34.9 %copy-start.11 = (f32[2,512]{1,0:T(2,128)S(1)}, f32[2,512]{1,0:T(2,128)}, u32[]{:S(2)}) copy-start(f32[2,512]{1,0:T(2,128)} %param.24) | copy-start | bytes 12292
  168.4 67.7 %all-gather.6.cloned.1.call-start = ((), (), s32[]{:S(2)}) async-start(), calls=%async_computation.5 | async-start | bytes 1310720 | tf_op jit(solution)/shard_map/all_gather | solution.py:63
  169.2 101.9 %reduce-scatter.6.cloned.1.call-start = ((), (), s32[]{:S(2)}) async-start(), calls=%async_computation.6 | async-start | bytes 655360 | tf_op jit(solution)/shard_map/reduce_scatter | solution.py:69
  201.2 34.9 %copy-start.1 = (f32[2,512,512]{2,1,0:T(8,128)S(1)}, f32[2,512,512]{2,1,0:T(8,128)}, u32[]{:S(2)}) copy-start(f32[2,512,512]{2,1,0:T(8,128)} %all-gather.4.cloned.1.call-done) | copy-start | bytes 6291460
  203.4 34.9 %copy-start.8 = (f32[2,512]{1,0:T(2,128)}, f32[2,512]{1,0:T(2,128)S(1)}, u32[]{:S(2)}) copy-start(f32[2,512]{1,0:T(2,128)S(1)} %get-tuple-element.56) | copy-start | bytes 12292
  203.4 34.9 %copy-start.9 = (f32[2,512]{1,0:T(2,128)}, f32[2,512]{1,0:T(2,128)S(1)}, u32[]{:S(2)}) copy-start(f32[2,512]{1,0:T(2,128)S(1)} %get-tuple-element.57) | copy-start | bytes 12292
  238.3 32.8 %copy-start.7 = (f32[32,1024]{1,0:T(8,128)S(1)}, f32[32,1024]{1,0:T(8,128)}, u32[]{:S(2)}) copy-start(f32[32,1024]{1,0:T(8,128)} %param.27) | copy-start | bytes 393220
  238.3 32.7 %copy-start.13 = (s32[128]{0:T(128)S(1)}, s32[128]{0:T(128)}, u32[]{:S(2)}) copy-start(s32[128]{0:T(128)} %copy-done.12) | copy-start | bytes 1540
  250.6 35.5 %copy-start.14 = (f32[2,8]{1,0:T(2,128)S(1)}, f32[2,8]{1,0:T(2,128)}, u32[]{:S(2)}) copy-start(f32[2,8]{1,0:T(2,128)} %param.31) | copy-start | bytes 196
  250.6 35.5 %copy-start.15 = (f32[2,8]{1,0:T(2,128)S(1)}, f32[2,8]{1,0:T(2,128)}, u32[]{:S(2)}) copy-start(f32[2,8]{1,0:T(2,128)} %param.32) | copy-start | bytes 196
  251.7 50.0 %all-to-all-start.1 = ((f32[2,512,128]{2,0,1:T(2,128)}), f32[2,512,128]{2,0,1:T(2,128)S(1)}, u32[]{:S(2)}, u32[]{:S(2)}) async-start(f32[2,512,128]{2,0,1:T(2,128)} %copy.65), calls=%async_computation.1 | async-start | bytes 1048576 | tf_op jit(solution)/shard_map/all_to_all | solution.py:103
  271.0 28.5 %copy-start.2 = (f32[1,2,128,4,128]{4,3,2,1,0:T(4,128)S(1)}, f32[1,2,128,4,128]{4,3,2,1,0:T(4,128)}, u32[]{:S(2)}) copy-start(f32[1,2,128,4,128]{4,3,2,1,0:T(4,128)} %copy.62) | copy-start | bytes 1572868
  295.4 4.1 %copy-start.4 = (f32[2,128,512]{2,1,0:T(8,128)S(1)}, f32[2,128,512]{2,1,0:T(8,128)}, u32[]{:S(2)}) copy-start(f32[2,128,512]{2,1,0:T(8,128)} %param.20) | copy-start | bytes 1572868
  301.7 1.6 copy-start.6
  302.1 15.1 %copy-start.3 = (bf16[32,4096]{1,0:T(8,128)(2,1)S(1)}, bf16[32,4096]{1,0:T(8,128)(2,1)}, u32[]{:S(2)}) copy-start(bf16[32,4096]{1,0:T(8,128)(2,1)} %all_gather.18) | copy-start | bytes 786436
Sparse Core Ops, SparseCore 0:
  64.2 35.4 reduce-scatter.7
  168.5 32.6 all-gather.3
  203.3 32.7 all-gather.5
  239.4 29.7 reduce-scatter.5
where the time goes:
time: 325 us; the launch traced here: 324 us
  waiting for transfers between devices  96.6 us (30%)
  blocking collectives  91.1 us (28%)
  local copies, waits for them, and re-layouts  83.5 us (26%)
  starting transfers between devices  16.8 us (5%)
  between operations  14.8 us (5%)
  other arithmetic  13.3 us (4%)
  matrix products  8.48 us (3%)
    unnamed x44, local copies, waits for them, and re-layouts  76.9 us
    all_to_all x1, blocking collectives, per_device(): lax.all_to_all(outgoing, 'shard', split_axis=0, concat_axis=2, tiled=True)  48.5 us
    unnamed x5, waiting for transfers between devices  34.7 us
    all_gather x1, waiting for transfers between devices, per_device(): left_full = lax.all_gather(left_roots, 'tensor', axis=1, tiled=True)  31.3 us
    all_gather x1, waiting for transfers between devices, per_device(): full_block = lax.all_gather(own_cols, 'tensor', axis=2, tiled=True)  30.6 us
    all_to_all x1, starting transfers between devices, per_device(): lax.all_to_all(update, 'shard', split_axis=1, concat_axis=0, tiled=True)  16.6 us
    all_gather x1, blocking collectives, per_device(): lax.all_gather(emb_low, 'tensor', axis=1, tiled=True)  13.1 us
    all_gather x1, blocking collectives, per_device(): lax.all_gather(wo_new.astype(jnp.bfloat16), 'tensor', axis=4, tiled=True)  12.2 us
  transfers between devices with their start and end apart: 5, of which 3 were waited for; matrix products, arithmetic and copies ran while one was open for 7% of the time, Pallas kernels for 0%

commit v1 on v0

--- a/solution.py
+++ b/solution.py
@@ -97,7 +97,11 @@
     ).astype(jnp.bfloat16)
     shampoo = jnp.einsum("sik,skq->siq", left_full, right_half, preferred_element_type=jnp.float32)
     shampoo_part = jnp.sum(shampoo * shampoo, axis=(1, 2))
-    shampoo_total = lax.psum(shampoo_part, "tensor")
+    shampoo_total = shampoo_part
+    for hop in (1, 2):
+        shampoo_total = shampoo_total + lax.ppermute(
+            shampoo_total, "tensor", [(dev, dev ^ hop) for dev in range(4)]
+        )
     graft_ratio = jnp.sqrt(adam_total) / (jnp.sqrt(shampoo_total) + graft_eps)
     update = shampoo * graft_ratio[:, None, None]
     returned = lax.all_to_all(update, "shard", split_axis=1, concat_axis=0, tiled=True)

time: 325 us -> 336 us (1.034)
  the two profiles are of different devices: /device:TPU:40 before, /device:TPU:34 now
where the time goes in v1:
time: 336 us; the launch traced here: 335 us
  waiting for transfers between devices  99.2 us (30%)
  blocking collectives  92.7 us (28%)
  local copies, waits for them, and re-layouts  82.4 us (25%)
  starting transfers between devices  23.2 us (7%)
  between operations  14.8 us (4%)
  other arithmetic  13.9 us (4%)
  matrix products  8.99 us (3%)
    unnamed x40, local copies, waits for them, and re-layouts  76.5 us
    all_to_all x1, blocking collectives, per_device(): lax.all_to_all(outgoing, 'shard', split_axis=0, concat_axis=2, tiled=True)  49.4 us
    unnamed x5, waiting for transfers between devices  33 us
    all_gather x1, waiting for transfers between devices, per_device(): full_block = lax.all_gather(own_cols, 'tensor', axis=2, tiled=True)  31.2 us
    all_gather x1, waiting for transfers between devices, per_device(): left_full = lax.all_gather(left_roots, 'tensor', axis=1, tiled=True)  30.8 us
    all_to_all x1, starting transfers between devices, per_device(): lax.all_to_all(update, 'shard', split_axis=1, concat_axis=0, tiled=True)  16.6 us
    all_gather x1, blocking collectives, per_device(): lax.all_gather(emb_low, 'tensor', axis=1, tiled=True)  12.1 us
    all_gather x1, blocking collectives, per_device(): lax.all_gather(wo_new.astype(jnp.bfloat16), 'tensor', axis=4, tiled=True)  12 us
  transfers between devices with their start and end apart: 7, of which 4 were waited for; matrix products, arithmetic and copies ran while one was open for 7% of the time, Pallas kernels for 0%

profile of v1, /device:TPU:34, one launch (start us, length us, event | category | flops | bytes accessed | tf_op | source)
XLA Modules:
  0.0 335.2 jit_solution(16844900734075884010)
XLA Ops:
  7.2 1.2 bitcast_convert_fusion
  8.5 26.2 %copy.74 = f32[2,8,8,4,512]{3,2,1,0,4:T(8,128)} copy(f32[2,8,8,4,512]{4,3,2,1,0:T(4,128)S(1)} %bitcast_convert_fusion) | data formatting | bytes 2097152
  34.7 29.3 %reshape.124 = f32[512,512]{1,0:T(8,128)} reshape(f32[512,2,8,8,4]{4,3,2,1,0:T(8,128)} %bitcast.45) | data formatting | bytes 2097152
  64.1 0.2 convert_reduce_fusion.1
  64.3 0.5 compare_and_fusion.1
  64.9 0.1 reduce_sum.79
  65.1 0.2 gt.18
  65.3 32.3 %reduce-scatter.8.cloned.1.call-done = f32[128,512]{1,0:T(8,128)} async-done(((f32[512,512]{1,0:T(8,128)}), f32[128,512]{1,0:T(8,128)}) %reduce-scatter.8.cloned.1.call-update) | async-done | bytes 262160
  97.6 10.8 %reshape.125 = f32[128,2,8,8,4]{4,3,2,1,0:T(8,128)} reshape(f32[128,512]{1,0:T(8,128)} %reduce-scatter.8.cloned.1.call-done) | data formatting | bytes 524288
  108.4 6.6 %copy.75 = f32[2,8,8,4,128]{4,3,2,1,0:T(4,128)S(1)} copy(f32[2,8,8,4,128]{3,2,1,0,4:T(8,128)} %bitcast.46) | data formatting | bytes 524288
  115.1 1.0 gather_fusion
  116.2 0.5 select_select_fusion
  116.7 0.2 copy.61
  116.9 49.4 %all_to_all.33 = f32[128,2,4,128]{3,1,2,0:T(2,128)S(1)} all-to-all(f32[128,2,4,128]{3,1,2,0:T(2,128)S(1)} %copy.61), channel_id=1, replica_groups=mesh['shard'=128,'tensor'=4] {'shard'}, dimensions={0} | all-to-all | bytes 1048576 | tf_op jit(solution)/shard_map/all_to_all | solution.py:78
  166.3 0.9 copy.62
  167.3 0.7 all-gather.6.cloned.1.call-update
  168.0 0.8 bitcast_convert_fusion.1
  168.9 0.6 bitcast_convert_fusion.2
  169.4 31.2 %all-gather.4.cloned.1.call-done = f32[2,512,512]{2,1,0:T(8,128)} async-done(((f32[2,512,128]{2,1,0:T(8,128)}), f32[2,512,512]{2,1,0:T(8,128)}) %all-gather.4.cloned.1.call-update) | async-done | bytes 2097168 | tf_op jit(solution)/shard_map/all_gather | solution.py:79
  200.7 2.0 multiply_reduce_fusion
  202.7 0.1 fusion.8
  202.9 0.9 copy.73
  203.7 0.5 broadcast_multiply_fusion.1
  204.2 30.8 %all-gather.6.cloned.1.call-done = bf16[2,512,512]{2,1,0:T(8,128)(2,1)} async-done(((bf16[2,128,512]{2,1,0:T(8,128)(2,1)}), bf16[2,512,512]{2,1,0:T(8,128)(2,1)}) %all-gather.6.cloned.1.call-update) | async-done | bytes 1048592 | tf_op jit(solution)/shard_map/all_gather | solution.py:63
  235.1 2.7 multiply_reduce_fusion.2
  237.8 2.3 multiply_reduce_fusion.3
  240.0 3.6 %collective-permute-start = (f32[2]{0:T(128)}, f32[2]{0:T(128)S(1)}, u32[]{:S(2)}, u32[]{:S(2)}) collective-permute-start(f32[2]{0:T(128)} %get-tuple-element.34), channel_id=1, source_target_pairs={{0,1},{1,0},{2,3},{3,2},{4,5},{5,4},{6,7},{7,6},{8,9},{9,8},{10,11... | collective-permute-start | bytes 32 | tf_op jit(solution)/shard_map/ppermute | solution.py:102
  243.6 8.7 %all-reduce.1 = (f32[2]{0:T(128)S(1)}, f32[2,32]{1,0:T(2,128)}) all-reduce(f32[2]{0:T(128)S(1)} %multiply_reduce_fusion.3, f32[2,32]{1,0:T(2,128)} %bitcast_convert_fusion.2), channel_id=1, replica_groups=mesh['shard'=128,'tensor'=4] {'tensor'}, use_global_device_ids=true, to_apply=%region_8.9 | all-reduce | flops 66 | bytes 528 | tf_op jit(solution)/shard_map/psum | solution.py:91
  252.4 0.7 add.121
  253.0 2.8 collective-permute-start.1
  255.8 4.2 %collective-permute-done.1 = f32[2]{0:T(128)S(1)} collective-permute-done((f32[2]{0:T(128)S(1)}, f32[2]{0:T(128)S(1)}, u32[]{:S(2)}, u32[]{:S(2)}) %collective-permute-start.1) | collective-permute-done | bytes 40 | tf_op jit(solution)/shard_map/ppermute | solution.py:102
  260.2 1.0 copy.65
  261.1 16.6 %all-to-all-start.1 = ((f32[2,512,128]{2,0,1:T(2,128)}), f32[2,512,128]{2,0,1:T(2,128)S(1)}, u32[]{:S(2)}, u32[]{:S(2)}) async-start(f32[2,512,128]{2,0,1:T(2,128)} %copy.65), calls=%async_computation.1 | async-start | bytes 1048576 | tf_op jit(solution)/shard_map/all_to_all | solution.py:107
  277.9 1.3 dynamic-slice
  279.9 1.9 fusion.6
  281.8 12.1 %all_gather.18 = bf16[32,4096]{1,0:T(8,128)(2,1)} all-gather(bf16[32,1024]{1,0:T(8,128)(2,1)S(1)} %get-tuple-element.24), channel_id=1, replica_groups=mesh['shard'=128,'tensor'=4] {'tensor'}, dimensions={1}, use_global_device_ids=true | all-gather | bytes 327680 | tf_op jit(solution)/shard_map/all_gather | solution.py:120
  293.9 1.4 convert_bitcast_fusion
  295.2 10.5 %all-gather = bf16[4,8,2]{1,2,0:T(2,128)(2,1)S(1)} all-gather(bf16[1,8,2]{1,2,0:T(2,128)(2,1)S(1)} %get-tuple-element.20), channel_id=1, replica_groups=mesh['shard'=128,'tensor'=4] {'tensor'}, dimensions={0}, use_global_device_ids=true | all-gather | bytes 160 | tf_op jit(solution)/shard_map/all_gather | solution.py:121
  305.7 0.6 reshape.123
  306.3 4.1 %convolution_add_fusion.1 = f32[2,128,512]{2,1,0:T(8,128)} fusion(f32[2,128,512]{2,1,0:T(8,128)} %param.19, f32[2,512,512]{2,1,0:T(8,128)S(1)} %copy-done.1, s32[]{:T(128)S(6)} %select_n.46), kind=kOutput, calls=%fused_computation.5 | convolution fusion | flops 805437440 | bytes 3670020 | tf_op jit(solution)/shard_map/sqj,sij->sqi/dot_general | solution.py:81
  310.5 2.2 convolution_add_fusion
  312.7 0.4 copy.67
  313.1 0.3 copy.68
  313.5 0.7 gather_fusion.1
  314.2 0.9 fusion.7
  315.2 12.0 %all_gather.17 = bf16[2,8,8,4,512]{4,3,2,1,0:T(4,128)(2,1)S(1)} all-gather(bf16[2,8,8,4,128]{4,3,2,1,0:T(4,128)(2,1)S(1)} %get-tuple-element.28), channel_id=1, replica_groups=mesh['shard'=128,'tensor'=4] {'tensor'}, dimensions={4}, use_global_device_ids=true | all-gather | bytes 655360 | tf_op jit(solution)/shard_map/all_gather | solution.py:119
  327.2 0.8 copy.80
  328.0 0.7 copy.81
  (57 shorter events, 0.8 us)
Async XLA Ops:
  7.2 227.9 %copy-start = (bf16[2,128,512]{2,1,0:T(8,128)(2,1)S(1)}, bf16[2,128,512]{2,1,0:T(8,128)(2,1)}, u32[]{:S(2)}) copy-start(bf16[2,128,512]{2,1,0:T(8,128)(2,1)} %param.22) | copy-start | bytes 786436
  7.2 90.4 %reduce-scatter.8.cloned.1.call-start = ((), (), s32[]{:S(2)}) async-start(), calls=%async_computation.7 | async-start | bytes 1310720
  34.7 29.4 %copy-start.14 = (s32[128]{0:T(128)S(1)}, s32[128]{0:T(128)}, u32[]{:S(2)}) copy-start(s32[128]{0:T(128)} %param.25) | copy-start | bytes 1540
  64.1 136.6 %all-gather.4.cloned.1.call-start = ((), (), s32[]{:S(2)}) async-start(), calls=%async_computation.4 | async-start | bytes 2621440 | tf_op jit(solution)/shard_map/all_gather | solution.py:79
  116.7 51.3 %copy-start.5 = (bf16[1,32,4096]{2,1,0:T(8,128)(2,1)S(1)}, bf16[1,32,4096]{2,1,0:T(8,128)(2,1)}, u32[]{:S(2)}) copy-start(bf16[1,32,4096]{2,1,0:T(8,128)(2,1)} %param.26) | copy-start | bytes 786436
  116.9 52.0 %copy-start.15 = (bf16[1,2,32]{2,1,0:T(2,128)(2,1)S(1)}, bf16[1,2,32]{2,1,0:T(2,128)(2,1)}, u32[]{:S(2)}) copy-start(bf16[1,2,32]{2,1,0:T(2,128)(2,1)} %param.30) | copy-start | bytes 388
  167.2 35.5 %copy-start.10 = (f32[2,512]{1,0:T(2,128)S(1)}, f32[2,512]{1,0:T(2,128)}, u32[]{:S(2)}) copy-start(f32[2,512]{1,0:T(2,128)} %param.23) | copy-start | bytes 12292
  167.2 35.5 %copy-start.11 = (f32[2,512]{1,0:T(2,128)S(1)}, f32[2,512]{1,0:T(2,128)}, u32[]{:S(2)}) copy-start(f32[2,512]{1,0:T(2,128)} %param.24) | copy-start | bytes 12292
  167.2 67.8 %all-gather.6.cloned.1.call-start = ((), (), s32[]{:S(2)}) async-start(), calls=%async_computation.5 | async-start | bytes 1310720 | tf_op jit(solution)/shard_map/all_gather | solution.py:63
  168.0 111.9 %reduce-scatter.6.cloned.1.call-start = ((), (), s32[]{:S(2)}) async-start(), calls=%async_computation.6 | async-start | bytes 655360 | tf_op jit(solution)/shard_map/reduce_scatter | solution.py:69
  200.7 34.4 %copy-start.1 = (f32[2,512,512]{2,1,0:T(8,128)S(1)}, f32[2,512,512]{2,1,0:T(8,128)}, u32[]{:S(2)}) copy-start(f32[2,512,512]{2,1,0:T(8,128)} %all-gather.4.cloned.1.call-done) | copy-start | bytes 6291460
  202.9 34.9 %copy-start.8 = (f32[2,512]{1,0:T(2,128)}, f32[2,512]{1,0:T(2,128)S(1)}, u32[]{:S(2)}) copy-start(f32[2,512]{1,0:T(2,128)S(1)} %get-tuple-element.55) | copy-start | bytes 12292
  202.9 34.9 %copy-start.9 = (f32[2,512]{1,0:T(2,128)}, f32[2,512]{1,0:T(2,128)S(1)}, u32[]{:S(2)}) copy-start(f32[2,512]{1,0:T(2,128)S(1)} %get-tuple-element.56) | copy-start | bytes 12292
  237.8 42.1 %copy-start.7 = (f32[32,1024]{1,0:T(8,128)S(1)}, f32[32,1024]{1,0:T(8,128)}, u32[]{:S(2)}) copy-start(f32[32,1024]{1,0:T(8,128)} %param.27) | copy-start | bytes 393220
  237.8 40.0 %copy-start.12 = (pred[128]{0:T(512)(128)(4,1)S(1)}, pred[128]{0:T(512)(128)(4,1)}, u32[]{:S(2)}) copy-start(pred[128]{0:T(512)(128)(4,1)} %get-tuple-element.30) | copy-start | bytes 388
  240.0 12.4 %collective-permute-start = (f32[2]{0:T(128)}, f32[2]{0:T(128)S(1)}, u32[]{:S(2)}, u32[]{:S(2)}) collective-permute-start(f32[2]{0:T(128)} %get-tuple-element.34), channel_id=1, source_target_pairs={{0,1},{1,0},{2,3},{3,2},{4,5},{5,4},{6,7},{7,6},{8,9},{9,8},{10,11... | collective-permute-start | bytes 32 | tf_op jit(solution)/shard_map/ppermute | solution.py:102
  253.0 7.0 %collective-permute-start.1 = (f32[2]{0:T(128)S(1)}, f32[2]{0:T(128)S(1)}, u32[]{:S(2)}, u32[]{:S(2)}) collective-permute-start(f32[2]{0:T(128)S(1)} %add.121), channel_id=1, source_target_pairs={{0,2},{1,3},{2,0},{3,1},{4,6},{5,7},{6,4},{7,5},{8,10},{9,11},{10,... | collective-permute-start | bytes 32 | tf_op jit(solution)/shard_map/ppermute | solution.py:102
  260.0 33.9 %copy-start.13 = (f32[2,8]{1,0:T(2,128)S(1)}, f32[2,8]{1,0:T(2,128)}, u32[]{:S(2)}) copy-start(f32[2,8]{1,0:T(2,128)} %param.31) | copy-start | bytes 196
  261.1 51.5 %all-to-all-start.1 = ((f32[2,512,128]{2,0,1:T(2,128)}), f32[2,512,128]{2,0,1:T(2,128)S(1)}, u32[]{:S(2)}, u32[]{:S(2)}) async-start(f32[2,512,128]{2,0,1:T(2,128)} %copy.65), calls=%async_computation.1 | async-start | bytes 1048576 | tf_op jit(solution)/shard_map/all_to_all | solution.py:107
  279.8 30.6 %copy-start.2 = (f32[1,2,128,4,128]{4,3,2,1,0:T(4,128)S(1)}, f32[1,2,128,4,128]{4,3,2,1,0:T(4,128)}, u32[]{:S(2)}) copy-start(f32[1,2,128,4,128]{4,3,2,1,0:T(4,128)} %copy.62) | copy-start | bytes 1572868
  306.3 4.1 %copy-start.4 = (f32[2,128,512]{2,1,0:T(8,128)S(1)}, f32[2,128,512]{2,1,0:T(8,128)}, u32[]{:S(2)}) copy-start(f32[2,128,512]{2,1,0:T(8,128)} %param.20) | copy-start | bytes 1572868
  312.7 1.6 copy-start.6
  313.1 14.8 %copy-start.3 = (bf16[32,4096]{1,0:T(8,128)(2,1)S(1)}, bf16[32,4096]{1,0:T(8,128)(2,1)}, u32[]{:S(2)}) copy-start(bf16[32,4096]{1,0:T(8,128)(2,1)} %all_gather.18) | copy-start | bytes 786436
Sparse Core Ops, SparseCore 0:
  64.2 33.3 reduce-scatter.7
  167.3 33.2 all-gather.3
  202.8 32.2 all-gather.5
  238.3 28.8 reduce-scatter.5
